TPU v7x, 32 devices: a whole 2x2x4 slice. The times are simulated.
32 devices in a mesh: req: 16 (over z, x, core), tp: 2 (over y).
Axes of the slice: x: 2, y: 2, z: 4, core: 2. Of those that a mesh axis runs over, the one named last changes fastest.
Arguments:
- x_in: bfloat16 [2048, 8192], P('req', 'tp'), may hold values from -6 to 6
- z_gate: bfloat16 [2048, 8192], P('req', 'tp'), may hold values from -6 to 6
- conv_edge: bfloat16 [128, 3, 8192], P('req', None, 'tp'), may hold values from -6 to 6
- conv_weight: float32 [4, 8192], P(None, 'tp'), may hold values from -3 to 3
- conv_bias: float32 [8192], P('tp'), may hold values from -3 to 3
- x_proj_weight: bfloat16 [8192, 288], P('tp'), may hold values from -0.0625 to 0.0625
- dt_gain: float32 [256], replicated, may hold values from 0.5 to 1.5
- b_gain: float32 [16], replicated, may hold values from 0.5 to 1.5
- c_gain: float32 [16], replicated, may hold values from 0.5 to 1.5
- dt_proj_weight: bfloat16 [256, 8192], P(None, 'tp'), may hold values from -0.375 to 0.375
- dt_bias: float32 [8192], P('tp'), may hold values from -6 to -2
- a_log: float32 [16, 8192], P(None, 'tp'), may hold values from 0 to 3
- skip: float32 [8192], P('tp'), may hold values from 0.5 to 1.5
- ssm_state: bfloat16 [128, 16, 8192], P('req', None, 'tp'), may hold values from -6 to 6
- accepted: int32 [128], P('req'), may hold values from 0 to 16, as said below
- prompt_len: int32 [128], P('req'), may hold values from 1 to 8192, 131072 in all
- tenant_range: int32 [4, 2], replicated, may hold values from 0 to 128, as said below
- owner: int32 [128], replicated, may hold values from 0 to 15, as said below
Outputs:
- mixed_out: bfloat16 [2048, 8192], P('req', 'tp')
- owned_state: bfloat16 [192, 16, 8192], P('req', None, 'tp')
- owned_edge: bfloat16 [192, 3, 8192], P('req', None, 'tp')
- tenant_stats: float32 [4, 2], replicated
Inputs may be any that keep to these rules, and one draw needn't show every extreme that they name: `accepted`: accepted draft tokens; the largest value 16 occurs in every draw. `tenant_range`: the rows cover all requests in order, row k starting where row k - 1 ends; every tenant has at least one request. The 8 requests of one device go to 8 different owners; at most 12 requests go to one owner, and some owner receives exactly 12 in every draw.
All inputs are finite; a program needn't handle non-finite values. No bound on the sum of `prompt_len` on one device may be relied on, other than what follows from the above.
Results may differ from a plain program's by a relative error of at most 0.0085.
Values may be sent and summed in bfloat16 or wider, within the bound.
No kernel may reach another device: no remote copies, remote signals or barrier semaphores. Data moves between devices by JAX's collectives and lax.ppermute only.
A program may use at most 64 MiB of HBM per device.

v0:
```python
import jax
import jax.numpy as jnp
from jax import lax
from jax.sharding import PartitionSpec as P

STEPS = 16
PAIR_MOST = 1
EPSILON = 1e-06
SQUARE_FLOOR = 0.25


def rms_scaled(values, scale_gain, floor_value, eps_value):
    square = jnp.mean(values * values, axis=-1, keepdims=True)
    return values * lax.rsqrt(jnp.maximum(square, floor_value) + eps_value) * scale_gain


def normalize(projected, dt_gain, b_gain, c_gain):
    rank_cols = dt_gain.shape[0]
    state_cols = b_gain.shape[0]
    dt_low = rms_scaled(projected[:, :rank_cols], dt_gain, 0.0, EPSILON).astype(jnp.bfloat16)
    input_map = rms_scaled(
        projected[:, rank_cols : rank_cols + state_cols], b_gain, SQUARE_FLOOR, 0.0
    ).astype(jnp.bfloat16)
    output_map = rms_scaled(
        projected[:, rank_cols + state_cols :], c_gain, SQUARE_FLOOR, 0.0
    ).astype(jnp.bfloat16)
    return (dt_low, input_map, output_map)


def per_device(
    x_in,
    z_gate,
    conv_edge,
    conv_weight,
    conv_bias,
    x_proj_weight,
    dt_gain,
    b_gain,
    c_gain,
    dt_proj_weight,
    dt_bias,
    a_log,
    skip,
    ssm_state,
    accepted,
    prompt_len,
    tenant_range,
    owner,
):
    per_dev = ssm_state.shape[0]
    channels = x_in.shape[1]
    drafts = x_in.shape[0] // per_dev
    taps = conv_weight.shape[0]
    state_size = ssm_state.shape[1]
    owners = lax.axis_size("req")
    device = lax.axis_index("req")
    own_most = min(per_dev + per_dev // 2, owners)
    window = jnp.concatenate([conv_edge, x_in.reshape(per_dev, drafts, channels)], axis=1)
    lag_index = accepted[:, None] + jnp.arange(taps - 1, dtype=jnp.int32)[None, :]
    kept_edge = jnp.take_along_axis(window, lag_index[:, :, None], axis=1)
    my_owners = lax.dynamic_slice_in_dim(owner, device * per_dev, per_dev)
    local_ids = jnp.arange(per_dev, dtype=jnp.int32)
    earlier = jnp.sum(
        (my_owners[None, :] == my_owners[:, None]) & (local_ids[None, :] < local_ids[:, None]),
        axis=1,
    )
    send_slot = my_owners * PAIR_MOST + earlier

    def place_rows(payload):
        blank_rows = jnp.zeros((owners * PAIR_MOST,) + payload.shape[1:], payload.dtype)
        return blank_rows.at[send_slot].set(payload)

    route_table = owner.reshape(owners, per_dev)
    incoming = jnp.sum((route_table == device).astype(jnp.int32), axis=1)
    occupied = (jnp.arange(PAIR_MOST, dtype=jnp.int32)[None, :] < incoming[:, None]).reshape(-1)
    target = jnp.where(occupied, jnp.cumsum(occupied.astype(jnp.int32)) - 1, own_most)

    def settle_rows(payload):
        blank_rows = jnp.zeros((own_most,) + payload.shape[1:], payload.dtype)
        return blank_rows.at[target].set(payload, mode="drop")

    summed = jnp.zeros((per_dev, drafts, channels), jnp.float32) + conv_bias
    for offset in range(taps):
        summed = summed + conv_weight[offset] * window[:, offset : offset + drafts, :].astype(
            jnp.float32
        )
    conv_out = jax.nn.silu(summed).astype(jnp.bfloat16)
    flattened = conv_out.reshape(per_dev * drafts, channels)
    partial_proj = jnp.dot(flattened, x_proj_weight, preferred_element_type=jnp.float32)
    projected = lax.psum(partial_proj, "tp")
    dt_low, input_map, output_map = normalize(projected, dt_gain, b_gain, c_gain)
    step_size = jax.nn.softplus(
        jnp.dot(dt_low, dt_proj_weight, preferred_element_type=jnp.float32) + dt_bias
    )
    step_size = step_size.reshape(per_dev, drafts, channels)
    decay_rate = -jnp.exp(a_log)
    conv_float = conv_out.astype(jnp.float32)
    in_float = input_map.astype(jnp.float32).reshape(per_dev, drafts, state_size)
    out_float = output_map.astype(jnp.float32).reshape(per_dev, drafts, state_size)
    initial = ssm_state.astype(jnp.float32)
    kept_first = jnp.where((accepted == 0)[:, None, None], initial, jnp.zeros_like(initial))

    def advance(running, position):
        hidden, kept_state = running
        size_now = step_size[:, position, :]
        conv_now = conv_float[:, position, :]
        decay_now = jnp.exp(size_now[:, None, :] * decay_rate[None, :, :])
        hidden = (
            decay_now * hidden + (size_now * conv_now)[:, None, :] * in_float[:, position, :, None]
        )
        output_now = jnp.sum(out_float[:, position, :, None] * hidden, axis=1) + skip * conv_now
        kept_state = jnp.where((accepted == position + 1)[:, None, None], hidden, kept_state)
        return ((hidden, kept_state), output_now)

    (last_state, kept_state), per_step = lax.scan(
        advance, (initial, kept_first), jnp.arange(drafts, dtype=jnp.int32)
    )
    kept_state = kept_state.astype(jnp.bfloat16)
    received_state, received_edge = (
        lax.all_to_all(place_rows(kept_state), "req", split_axis=0, concat_axis=0, tiled=True),
        lax.all_to_all(place_rows(kept_edge), "req", split_axis=0, concat_axis=0, tiled=True),
    )
    scan_out = jnp.transpose(per_step, (1, 0, 2))
    gate_float = z_gate.reshape(per_dev, drafts, channels).astype(jnp.float32)
    mixed_out = (
        (scan_out * jax.nn.silu(gate_float))
        .astype(jnp.bfloat16)
        .reshape(per_dev * drafts, channels)
    )
    owned_state = settle_rows(received_state)
    owned_edge = settle_rows(received_edge)
    global_ids = device * per_dev + local_ids
    inside = (global_ids[None, :] >= tenant_range[:, 0:1]) & (
        global_ids[None, :] < tenant_range[:, 1:2]
    )
    accepted_float = accepted.astype(jnp.float32)
    new_length = (prompt_len + accepted + 1).astype(jnp.float32)
    accept_sum = jnp.sum(jnp.where(inside, accepted_float[None, :], 0.0), axis=1)
    length_sum = jnp.sum(jnp.where(inside, new_length[None, :], 0.0), axis=1)
    partial_sums = jnp.stack([accept_sum, length_sum], axis=1)
    totals = lax.psum(partial_sums, "req")
    members = (tenant_range[:, 1] - tenant_range[:, 0]).astype(jnp.float32)
    accept_rate = totals[:, 0] / (STEPS * members)
    length_load = totals[:, 1] / members / (jnp.sum(totals[:, 1]) / jnp.sum(members))
    tenant_stats = jnp.stack([accept_rate, length_load], axis=1)
    return (mixed_out, owned_state, owned_edge, tenant_stats)


def solution(mesh):
    placed = (
        P("req", "tp"),
        P("req", "tp"),
        P("req", None, "tp"),
        P(None, "tp"),
        P("tp"),
        P("tp", None),
        P(),
        P(),
        P(),
        P(None, "tp"),
        P("tp"),
        P(None, "tp"),
        P("tp"),
        P("req", None, "tp"),
        P("req"),
        P("req"),
        P(),
        P(),
    )
    return jax.shard_map(
        per_device,
        mesh=mesh,
        in_specs=placed,
        out_specs=(P("req", "tp"), P("req", None, "tp"), P("req", None, "tp"), P()),
        check_vma=False,
    )
```

profile of v0, /device:TPU:16, one launch (start us, length us, event | category | flops | bytes accessed | tf_op | source)
XLA Modules:
  0.0 362.7 jit_solution(11368662169548580320)
XLA Ops:
  22.2 6.1 %all-to-all-start.1 = ((bf16[16,3,4096]{2,1,0:T(4,128)(2,1)}), bf16[16,3,4096]{2,1,0:T(4,128)(2,1)}, u32[]{:S(2)}, u32[]{:S(2)}) async-start(bf16[16,3,4096]{2,1,0:T(4,128)(2,1)} %scatter_fusion.2), calls=%async_computation.1 | async-start | bytes 1048576 | tf_op jit(solution)/shard_map/all_to_all | solution.py:121
  32.0 6.9 %all-reduce.2.cloned.1.call-done = f32[128,288]{0,1:T(8,128)} async-done(((f32[128,288]{0,1:T(8,128)}), f32[128,288]{0,1:T(8,128)}) %all-reduce.2.cloned.1.call-update) | async-done | bytes 147472 | tf_op jit(solution)/shard_map/psum | solution.py:90
  42.4 4.5 %compare_select_fusion = f32[128,4096]{1,0:T(8,128)} fusion(bf16[256,4096]{1,0:T(8,128)(2,1)} %param.29, f32[4096]{0:T(1024)} %param.30, f32[128,288]{0,1:T(8,128)} %all-reduce.2.cloned.1.call-done, f32[256]{0:T(256)} %param.26, f32[128]{0:T(128)S(1)} %add_rsqrt_fusion), kind=kOutput, calls=%fused_computation.17 | convolution fusion | flops 272203776 | bytes 4343296 | tf_op jit(solution)/shard_map/dot_general | solution.py:93
  47.0 212.8 %while.14 = (s32[]{:T(128)}, f32[8,16,4096]{2,1,0:T(8,128)}, bf16[8,16,4096]{2,1,0:T(8,128)(2,1)S(1)}, f32[16,8,4096]{2,1,0:T(8,128)}, s32[16]{0:T(128)S(1)}, /*...) while((s32[]{:T(128)}, f32[8,16,4096]{2,1,0:T(8,128)}, ...), condition=%wide.region_6.7_spmd, body=%wide.region_4.6_spmd.sunk | while | flops 3735566 | bytes 10243851 | solution.py:115
  52.5 3.5 multiply_reduce_fusion.5
  65.8 3.5 multiply_reduce_fusion.5
  79.1 3.5 multiply_reduce_fusion.5
  92.4 3.5 multiply_reduce_fusion.5
  105.7 3.5 multiply_reduce_fusion.5
  119.0 3.5 multiply_reduce_fusion.5
  132.3 3.5 multiply_reduce_fusion.5
  145.6 3.5 multiply_reduce_fusion.5
  158.9 3.5 multiply_reduce_fusion.5
  172.2 3.5 multiply_reduce_fusion.5
  185.5 3.5 multiply_reduce_fusion.5
  198.8 3.5 multiply_reduce_fusion.5
  212.1 3.5 multiply_reduce_fusion.5
  225.4 3.5 multiply_reduce_fusion.5
  238.7 3.5 multiply_reduce_fusion.5
  252.0 3.5 multiply_reduce_fusion.5
  264.2 6.2 %all-to-all-start = ((bf16[16,16,4096]{2,1,0:T(8,128)(2,1)}), bf16[16,16,4096]{2,1,0:T(8,128)(2,1)}, u32[]{:S(2)}, u32[]{:S(2)}) async-start(bf16[16,16,4096]{2,1,0:T(8,128)(2,1)} %scatter_fusion), calls=%async_computation | async-start | bytes 4194304 | tf_op jit(solution)/shard_map/all_to_all | solution.py:120
  270.7 65.5 %psum.15 = f32[4,2]{0,1:T(2,128)S(1)} all-reduce(f32[4,2]{0,1:T(2,128)S(1)} %pad_maximum_fusion), channel_id=1, replica_groups=mesh['req'=16,'tp'=2] {'req'}, use_global_device_ids=true, to_apply=%region_16.17 | all-reduce | flops 8 | bytes 64 | tf_op jit(solution)/shard_map/psum | solution.py:141
  341.4 3.6 fusion.2
  350.1 5.8 %scatter_fusion.1 = bf16[12,16,4096]{2,1,0:T(8,128)(2,1)} fusion(bf16[12,16,4096]{2,1,0:T(8,128)(2,1)} %broadcast_in_dim.97, s32[16]{0:T(128)S(1)} %fusion.5, bf16[16,16,4096]{2,1,0:T(8,128)(2,1)} %all-to-all-done), kind=kCustom, calls=%fused_computation.2 | custom fusion | bytes 6291520 | tf_op jit(solution)/shard_map/scatter | solution.py:80
  (201 shorter events, 150.2 us)
Async XLA Ops:
  7.2 7.3 %copy-start = (bf16[4096,288]{0,1:T(8,128)(2,1)S(1)}, bf16[4096,288]{0,1:T(8,128)(2,1)}, u32[]{:S(2)}) copy-start(bf16[4096,288]{0,1:T(8,128)(2,1)} %param.25) | copy-start | bytes 7077892
  7.2 4.0 %copy-start.2 = (bf16[128,4096]{1,0:T(8,128)(2,1)S(1)}, bf16[128,4096]{1,0:T(8,128)(2,1)}, u32[]{:S(2)}) copy-start(bf16[128,4096]{1,0:T(8,128)(2,1)} %param.20) | copy-start | bytes 3145732
  7.2 4.0 %copy-start.7 = (f32[4096]{0:T(1024)S(1)}, f32[4096]{0:T(1024)}, u32[]{:S(2)}) copy-start(f32[4096]{0:T(1024)} %param.24) | copy-start | bytes 49156
  7.2 31.7 %all-reduce.2.cloned.1.call-start = ((), (), s32[]{:S(2)}) async-start(), calls=%async_computation.2 | async-start | bytes 294912 | tf_op jit(solution)/shard_map/psum | solution.py:90
  11.2 2.7 copy-start.1
  14.4 1.5 copy-start.9
  14.5 1.7 copy-start.13
  22.2 242.1 %all-to-all-start.1 = ((bf16[16,3,4096]{2,1,0:T(4,128)(2,1)}), bf16[16,3,4096]{2,1,0:T(4,128)(2,1)}, u32[]{:S(2)}, u32[]{:S(2)}) async-start(bf16[16,3,4096]{2,1,0:T(4,128)(2,1)} %scatter_fusion.2), calls=%async_computation.1 | async-start | bytes 1048576 | tf_op jit(solution)/shard_map/all_to_all | solution.py:121
  28.3 2.9 copy-start.6
  28.3 11.4 %copy-start.10 = (f32[16]{0:T(128)S(1)}, f32[16]{0:T(128)}, u32[]{:S(2)}) copy-start(f32[16]{0:T(128)} %param.28) | copy-start | bytes 196
  28.3 11.3 %copy-start.11 = (f32[16]{0:T(128)S(1)}, f32[16]{0:T(128)}, u32[]{:S(2)}) copy-start(f32[16]{0:T(128)} %param.27) | copy-start | bytes 196
  42.4 4.6 %copy-start.5 = (f32[4096]{0:T(1024)S(1)}, f32[4096]{0:T(1024)}, u32[]{:S(2)}) copy-start(f32[4096]{0:T(1024)} %param.32) | copy-start | bytes 49156
  264.2 6.2 %copy-start.8 = (s32[4,2]{0,1:T(2,128)S(1)}, s32[4,2]{0,1:T(2,128)}, u32[]{:S(2)}) copy-start(s32[4,2]{0,1:T(2,128)} %param.36) | copy-start | bytes 100
  264.2 6.2 %copy-start.12 = (s32[8]{0:T(128)S(1)}, s32[8]{0:T(128)}, u32[]{:S(2)}) copy-start(s32[8]{0:T(128)} %param.35) | copy-start | bytes 100
  264.2 72.0 %copy-start.14 = (s32[128]{0:T(128)S(1)}, s32[128]{0:T(128)}, u32[]{:S(2)}) copy-start(s32[128]{0:T(128)} %param.37) | copy-start | bytes 1540
  264.2 72.4 %copy-start.4 = (bf16[128,4096]{1,0:T(8,128)(2,1)S(1)}, bf16[128,4096]{1,0:T(8,128)(2,1)}, u32[]{:S(2)}) copy-start(bf16[128,4096]{1,0:T(8,128)(2,1)} %param.21) | copy-start | bytes 3145732
  264.2 84.6 %all-to-all-start = ((bf16[16,16,4096]{2,1,0:T(8,128)(2,1)}), bf16[16,16,4096]{2,1,0:T(8,128)(2,1)}, u32[]{:S(2)}, u32[]{:S(2)}) async-start(bf16[16,16,4096]{2,1,0:T(8,128)(2,1)} %scatter_fusion), calls=%async_computation | async-start | bytes 4194304 | tf_op jit(solution)/shard_map/all_to_all | solution.py:120
  348.8 7.1 %copy-start.3 = (bf16[12,3,4096]{2,1,0:T(4,128)(2,1)}, bf16[12,3,4096]{2,1,0:T(4,128)(2,1)S(1)}, u32[]{:S(2)}) copy-start(bf16[12,3,4096]{2,1,0:T(4,128)(2,1)S(1)} %scatter_fusion.3) | copy-start | bytes 884740
Sparse Core Ops, SparseCore 0:
  16.1 22.7 all-reduce.1
where the time goes:
time: 367 us; the launch traced here: 363 us
  other arithmetic  146 us (40%)
  local copies, waits for them, and re-layouts  68.9 us (19%)
  blocking collectives  65.5 us (18%)
  loops' own time  41.6 us (11%)
  between operations  15.7 us (4%)
  starting transfers between devices  12.3 us (3%)
  waiting for transfers between devices  6.96 us (2%)
  matrix products  5.99 us (2%)
    psum x1, blocking collectives, per_device(): totals = lax.psum(partial_sums, 'req')  65.5 us
    reduce_sum x16, other arithmetic, advance(): jnp.sum(out_float[:, position, :, None] * hidden, axis=1) + skip * conv_now  56.6 us
    another operation x1, loops' own time, per_device(): lax.scan(advance, (initial, kept_first), jnp.arange(drafts, dtype=jnp.int...  41.6 us
    select_n x16, other arithmetic, advance(): jnp.where((accepted == position + 1)[:, None, None], hidden, kept_state)  31 us
    dynamic_update_slice x16, other arithmetic, per_device(): lax.scan(advance, (initial, kept_first), jnp.arange(drafts, dtype=jnp.int...  25.2 us
    dynamic_slice x16, local copies, waits for them, and re-layouts, advance(): size_now = step_size[:, position, :]  21.2 us
    mul x16, other arithmetic, advance(): decay_now = jnp.exp(size_now[:, None, :] * decay_rate[None, :, :])  16 us
    mul x16, local copies, waits for them, and re-layouts, advance(): out_float[:, position, :, None] * hidden  11.1 us
  transfers between devices with their start and end apart: 3, of which 1 were waited for; matrix products, arithmetic and copies ran while one was open for 56% of the time, Pallas kernels for 0%

commit v1 on v0

--- a/solution.py
+++ b/solution.py
@@ -7,6 +7,14 @@
 PAIR_MOST = 1
 EPSILON = 1e-06
 SQUARE_FLOOR = 0.25
+
+
+def added_up(block, mesh_axis):
+    size, result = (lax.axis_size(mesh_axis), block)
+    for reach in [1 << k for k in range(size.bit_length() - 1)]:
+        swap = [(i, i ^ reach) for i in range(size)]
+        result = result + lax.ppermute(result, mesh_axis, swap)
+    return result
 
 
 def rms_scaled(values, scale_gain, floor_value, eps_value):
@@ -138,7 +146,7 @@
     accept_sum = jnp.sum(jnp.where(inside, accepted_float[None, :], 0.0), axis=1)
     length_sum = jnp.sum(jnp.where(inside, new_length[None, :], 0.0), axis=1)
     partial_sums = jnp.stack([accept_sum, length_sum], axis=1)
-    totals = lax.psum(partial_sums, "req")
+    totals = added_up(partial_sums, "req")
     members = (tenant_range[:, 1] - tenant_range[:, 0]).astype(jnp.float32)
     accept_rate = totals[:, 0] / (STEPS * members)
     length_load = totals[:, 1] / members / (jnp.sum(totals[:, 1]) / jnp.sum(members))

time: 367 us -> 349 us (0.951)
  the two profiles are of different devices: /device:TPU:16 before, /device:TPU:0 now
where the time goes in v1:
time: 349 us; the launch traced here: 345 us
  other arithmetic  146 us (42%)
  local copies, waits for them, and re-layouts  68.7 us (20%)
  waiting for transfers between devices  46.4 us (13%)
  loops' own time  41.6 us (12%)
  starting transfers between devices  20.3 us (6%)
  between operations  15.7 us (4%)
  matrix products  5.99 us (2%)
    reduce_sum x16, other arithmetic, advance(): jnp.sum(out_float[:, position, :, None] * hidden, axis=1) + skip * conv_now  56.6 us
    another operation x1, loops' own time, per_device(): lax.scan(advance, (initial, kept_first), jnp.arange(drafts, dtype=jnp.int...  41.6 us
    ppermute x4, waiting for transfers between devices, added_up(): result = result + lax.ppermute(result, mesh_axis, swap)  39.1 us
    select_n x16, other arithmetic, advance(): jnp.where((accepted == position + 1)[:, None, None], hidden, kept_state)  31 us
    dynamic_update_slice x16, other arithmetic, per_device(): lax.scan(advance, (initial, kept_first), jnp.arange(drafts, dtype=jnp.int...  25.2 us
    dynamic_slice x16, local copies, waits for them, and re-layouts, advance(): size_now = step_size[:, position, :]  21.2 us
    mul x16, other arithmetic, advance(): decay_now = jnp.exp(size_now[:, None, :] * decay_rate[None, :, :])  16 us
    mul x16, local copies, waits for them, and re-layouts, advance(): out_float[:, position, :, None] * hidden  11.1 us
  transfers between devices with their start and end apart: 7, of which 4 were waited for; matrix products, arithmetic and copies ran while one was open for 59% of the time, Pallas kernels for 0%

profile of v1, /device:TPU:0, one launch (start us, length us, event | category | flops | bytes accessed | tf_op | source)
XLA Modules:
  0.0 344.5 jit_solution(13394112378421166936)
XLA Ops:
  22.1 7.4 %all-to-all-start.1 = ((bf16[16,3,4096]{2,1,0:T(4,128)(2,1)}), bf16[16,3,4096]{2,1,0:T(4,128)(2,1)}, u32[]{:S(2)}, u32[]{:S(2)}) async-start(bf16[16,3,4096]{2,1,0:T(4,128)(2,1)} %scatter_fusion.2), calls=%async_computation.1 | async-start | bytes 1048576 | tf_op jit(solution)/shard_map/all_to_all | solution.py:129
  33.2 7.3 %all-reduce.2.cloned.1.call-done = f32[128,288]{0,1:T(8,128)} async-done(((f32[128,288]{0,1:T(8,128)}), f32[128,288]{0,1:T(8,128)}) %all-reduce.2.cloned.1.call-update) | async-done | bytes 147472 | tf_op jit(solution)/shard_map/psum | solution.py:98
  44.0 4.5 %compare_select_fusion = f32[128,4096]{1,0:T(8,128)} fusion(bf16[256,4096]{1,0:T(8,128)(2,1)} %param.29, f32[4096]{0:T(1024)} %param.30, f32[128,288]{0,1:T(8,128)} %all-reduce.2.cloned.1.call-done, f32[256]{0:T(256)} %param.26, f32[128]{0:T(128)S(1)} %add_rsqrt_fusion), kind=kOutput, calls=%fused_computation.17 | convolution fusion | flops 272203776 | bytes 4343296 | tf_op jit(solution)/shard_map/dot_general | solution.py:101
  48.6 212.8 %while.14 = (s32[]{:T(128)}, f32[8,16,4096]{2,1,0:T(8,128)}, bf16[8,16,4096]{2,1,0:T(8,128)(2,1)S(1)}, f32[16,8,4096]{2,1,0:T(8,128)}, s32[16]{0:T(128)S(1)}, /*...) while((s32[]{:T(128)}, f32[8,16,4096]{2,1,0:T(8,128)}, ...), condition=%wide.region_6.7_spmd, body=%wide.region_4.6_spmd.sunk | while | flops 3735566 | bytes 10243851 | solution.py:123
  54.2 3.5 %multiply_reduce_fusion.5 = (f32[8,4096]{1,0:T(8,128)S(1)}, f32[8,16,4096]{2,1,0:T(8,128)}) fusion(f32[8,16]{1,0:T(8,128)S(1)} %get-tuple-element.238, f32[8,16]{1,0:T(8,128)S(1)} %get-tuple-element.239, f32[8,4096]{1,0:T(8,128)S(1)} %get-tuple-element.240, f32[8,16,4096]{2,1,0:T(8,128)} %get-tuple-element.260, f32[16,4096]{1,0:T(8,128)} %get-tuple-element.280, ...), kind=kLoop, calls=%fused_computation.5.clone.1 | loop fusion | flops 3112960 | bytes 4850688 | tf_op jit(solution)/shard_map/while/body/eval_jaxpr/reduce_sum | solution.py:119
  67.5 3.5 %multiply_reduce_fusion.5 = (f32[8,4096]{1,0:T(8,128)S(1)}, f32[8,16,4096]{2,1,0:T(8,128)}) fusion(f32[8,16]{1,0:T(8,128)S(1)} %get-tuple-element.238, f32[8,16]{1,0:T(8,128)S(1)} %get-tuple-element.239, f32[8,4096]{1,0:T(8,128)S(1)} %get-tuple-element.240, f32[8,16,4096]{2,1,0:T(8,128)} %get-tuple-element.260, f32[16,4096]{1,0:T(8,128)} %get-tuple-element.280, ...), kind=kLoop, calls=%fused_computation.5.clone.1 | loop fusion | flops 3112960 | bytes 4850688 | tf_op jit(solution)/shard_map/while/body/eval_jaxpr/reduce_sum | solution.py:119
  80.8 3.5 %multiply_reduce_fusion.5 = (f32[8,4096]{1,0:T(8,128)S(1)}, f32[8,16,4096]{2,1,0:T(8,128)}) fusion(f32[8,16]{1,0:T(8,128)S(1)} %get-tuple-element.238, f32[8,16]{1,0:T(8,128)S(1)} %get-tuple-element.239, f32[8,4096]{1,0:T(8,128)S(1)} %get-tuple-element.240, f32[8,16,4096]{2,1,0:T(8,128)} %get-tuple-element.260, f32[16,4096]{1,0:T(8,128)} %get-tuple-element.280, ...), kind=kLoop, calls=%fused_computation.5.clone.1 | loop fusion | flops 3112960 | bytes 4850688 | tf_op jit(solution)/shard_map/while/body/eval_jaxpr/reduce_sum | solution.py:119
  94.1 3.5 %multiply_reduce_fusion.5 = (f32[8,4096]{1,0:T(8,128)S(1)}, f32[8,16,4096]{2,1,0:T(8,128)}) fusion(f32[8,16]{1,0:T(8,128)S(1)} %get-tuple-element.238, f32[8,16]{1,0:T(8,128)S(1)} %get-tuple-element.239, f32[8,4096]{1,0:T(8,128)S(1)} %get-tuple-element.240, f32[8,16,4096]{2,1,0:T(8,128)} %get-tuple-element.260, f32[16,4096]{1,0:T(8,128)} %get-tuple-element.280, ...), kind=kLoop, calls=%fused_computation.5.clone.1 | loop fusion | flops 3112960 | bytes 4850688 | tf_op jit(solution)/shard_map/while/body/eval_jaxpr/reduce_sum | solution.py:119
  107.4 3.5 %multiply_reduce_fusion.5 = (f32[8,4096]{1,0:T(8,128)S(1)}, f32[8,16,4096]{2,1,0:T(8,128)}) fusion(f32[8,16]{1,0:T(8,128)S(1)} %get-tuple-element.238, f32[8,16]{1,0:T(8,128)S(1)} %get-tuple-element.239, f32[8,4096]{1,0:T(8,128)S(1)} %get-tuple-element.240, f32[8,16,4096]{2,1,0:T(8,128)} %get-tuple-element.260, f32[16,4096]{1,0:T(8,128)} %get-tuple-element.280, ...), kind=kLoop, calls=%fused_computation.5.clone.1 | loop fusion | flops 3112960 | bytes 4850688 | tf_op jit(solution)/shard_map/while/body/eval_jaxpr/reduce_sum | solution.py:119
  120.7 3.5 %multiply_reduce_fusion.5 = (f32[8,4096]{1,0:T(8,128)S(1)}, f32[8,16,4096]{2,1,0:T(8,128)}) fusion(f32[8,16]{1,0:T(8,128)S(1)} %get-tuple-element.238, f32[8,16]{1,0:T(8,128)S(1)} %get-tuple-element.239, f32[8,4096]{1,0:T(8,128)S(1)} %get-tuple-element.240, f32[8,16,4096]{2,1,0:T(8,128)} %get-tuple-element.260, f32[16,4096]{1,0:T(8,128)} %get-tuple-element.280, ...), kind=kLoop, calls=%fused_computation.5.clone.1 | loop fusion | flops 3112960 | bytes 4850688 | tf_op jit(solution)/shard_map/while/body/eval_jaxpr/reduce_sum | solution.py:119
  134.0 3.5 %multiply_reduce_fusion.5 = (f32[8,4096]{1,0:T(8,128)S(1)}, f32[8,16,4096]{2,1,0:T(8,128)}) fusion(f32[8,16]{1,0:T(8,128)S(1)} %get-tuple-element.238, f32[8,16]{1,0:T(8,128)S(1)} %get-tuple-element.239, f32[8,4096]{1,0:T(8,128)S(1)} %get-tuple-element.240, f32[8,16,4096]{2,1,0:T(8,128)} %get-tuple-element.260, f32[16,4096]{1,0:T(8,128)} %get-tuple-element.280, ...), kind=kLoop, calls=%fused_computation.5.clone.1 | loop fusion | flops 3112960 | bytes 4850688 | tf_op jit(solution)/shard_map/while/body/eval_jaxpr/reduce_sum | solution.py:119
  147.3 3.5 %multiply_reduce_fusion.5 = (f32[8,4096]{1,0:T(8,128)S(1)}, f32[8,16,4096]{2,1,0:T(8,128)}) fusion(f32[8,16]{1,0:T(8,128)S(1)} %get-tuple-element.238, f32[8,16]{1,0:T(8,128)S(1)} %get-tuple-element.239, f32[8,4096]{1,0:T(8,128)S(1)} %get-tuple-element.240, f32[8,16,4096]{2,1,0:T(8,128)} %get-tuple-element.260, f32[16,4096]{1,0:T(8,128)} %get-tuple-element.280, ...), kind=kLoop, calls=%fused_computation.5.clone.1 | loop fusion | flops 3112960 | bytes 4850688 | tf_op jit(solution)/shard_map/while/body/eval_jaxpr/reduce_sum | solution.py:119
  160.6 3.5 %multiply_reduce_fusion.5 = (f32[8,4096]{1,0:T(8,128)S(1)}, f32[8,16,4096]{2,1,0:T(8,128)}) fusion(f32[8,16]{1,0:T(8,128)S(1)} %get-tuple-element.238, f32[8,16]{1,0:T(8,128)S(1)} %get-tuple-element.239, f32[8,4096]{1,0:T(8,128)S(1)} %get-tuple-element.240, f32[8,16,4096]{2,1,0:T(8,128)} %get-tuple-element.260, f32[16,4096]{1,0:T(8,128)} %get-tuple-element.280, ...), kind=kLoop, calls=%fused_computation.5.clone.1 | loop fusion | flops 3112960 | bytes 4850688 | tf_op jit(solution)/shard_map/while/body/eval_jaxpr/reduce_sum | solution.py:119
  173.9 3.5 %multiply_reduce_fusion.5 = (f32[8,4096]{1,0:T(8,128)S(1)}, f32[8,16,4096]{2,1,0:T(8,128)}) fusion(f32[8,16]{1,0:T(8,128)S(1)} %get-tuple-element.238, f32[8,16]{1,0:T(8,128)S(1)} %get-tuple-element.239, f32[8,4096]{1,0:T(8,128)S(1)} %get-tuple-element.240, f32[8,16,4096]{2,1,0:T(8,128)} %get-tuple-element.260, f32[16,4096]{1,0:T(8,128)} %get-tuple-element.280, ...), kind=kLoop, calls=%fused_computation.5.clone.1 | loop fusion | flops 3112960 | bytes 4850688 | tf_op jit(solution)/shard_map/while/body/eval_jaxpr/reduce_sum | solution.py:119
  187.2 3.5 %multiply_reduce_fusion.5 = (f32[8,4096]{1,0:T(8,128)S(1)}, f32[8,16,4096]{2,1,0:T(8,128)}) fusion(f32[8,16]{1,0:T(8,128)S(1)} %get-tuple-element.238, f32[8,16]{1,0:T(8,128)S(1)} %get-tuple-element.239, f32[8,4096]{1,0:T(8,128)S(1)} %get-tuple-element.240, f32[8,16,4096]{2,1,0:T(8,128)} %get-tuple-element.260, f32[16,4096]{1,0:T(8,128)} %get-tuple-element.280, ...), kind=kLoop, calls=%fused_computation.5.clone.1 | loop fusion | flops 3112960 | bytes 4850688 | tf_op jit(solution)/shard_map/while/body/eval_jaxpr/reduce_sum | solution.py:119
  200.5 3.5 %multiply_reduce_fusion.5 = (f32[8,4096]{1,0:T(8,128)S(1)}, f32[8,16,4096]{2,1,0:T(8,128)}) fusion(f32[8,16]{1,0:T(8,128)S(1)} %get-tuple-element.238, f32[8,16]{1,0:T(8,128)S(1)} %get-tuple-element.239, f32[8,4096]{1,0:T(8,128)S(1)} %get-tuple-element.240, f32[8,16,4096]{2,1,0:T(8,128)} %get-tuple-element.260, f32[16,4096]{1,0:T(8,128)} %get-tuple-element.280, ...), kind=kLoop, calls=%fused_computation.5.clone.1 | loop fusion | flops 3112960 | bytes 4850688 | tf_op jit(solution)/shard_map/while/body/eval_jaxpr/reduce_sum | solution.py:119
  213.8 3.5 %multiply_reduce_fusion.5 = (f32[8,4096]{1,0:T(8,128)S(1)}, f32[8,16,4096]{2,1,0:T(8,128)}) fusion(f32[8,16]{1,0:T(8,128)S(1)} %get-tuple-element.238, f32[8,16]{1,0:T(8,128)S(1)} %get-tuple-element.239, f32[8,4096]{1,0:T(8,128)S(1)} %get-tuple-element.240, f32[8,16,4096]{2,1,0:T(8,128)} %get-tuple-element.260, f32[16,4096]{1,0:T(8,128)} %get-tuple-element.280, ...), kind=kLoop, calls=%fused_computation.5.clone.1 | loop fusion | flops 3112960 | bytes 4850688 | tf_op jit(solution)/shard_map/while/body/eval_jaxpr/reduce_sum | solution.py:119
  265.8 5.9 %all-to-all-start = ((bf16[16,16,4096]{2,1,0:T(8,128)(2,1)}), bf16[16,16,4096]{2,1,0:T(8,128)(2,1)}, u32[]{:S(2)}, u32[]{:S(2)}) async-start(bf16[16,16,4096]{2,1,0:T(8,128)(2,1)} %scatter_fusion), calls=%async_computation | async-start | bytes 4194304 | tf_op jit(solution)/shard_map/all_to_all | solution.py:128
  276.8 7.4 %collective-permute-done.1 = f32[4,2]{0,1:T(2,128)S(1)} collective-permute-done((f32[4,2]{0,1:T(2,128)S(1)}, f32[4,2]{0,1:T(2,128)S(1)}, u32[]{:S(2)}, u32[]{:S(2)}) %collective-permute-start.1) | collective-permute-done | bytes 64 | tf_op jit(solution)/shard_map/ppermute | solution.py:16
  284.8 21.9 %collective-permute-done.2 = f32[4,2]{0,1:T(2,128)S(1)} collective-permute-done((f32[4,2]{0,1:T(2,128)S(1)}, f32[4,2]{0,1:T(2,128)S(1)}, u32[]{:S(2)}, u32[]{:S(2)}) %collective-permute-start.2) | collective-permute-done | bytes 64 | tf_op jit(solution)/shard_map/ppermute | solution.py:16
  306.7 4.3 %collective-permute-start.3 = (f32[4,2]{0,1:T(2,128)S(1)}, f32[4,2]{0,1:T(2,128)S(1)}, u32[]{:S(2)}, u32[]{:S(2)}) collective-permute-start(f32[4,2]{0,1:T(2,128)S(1)} %add.205), channel_id=1, source_target_pairs={{0,16},{2,18},{4,20},{6,22},{8,24},{10,26},{12,28},{14,30},{16,0},... | collective-permute-start | bytes 104 | tf_op jit(solution)/shard_map/ppermute | solution.py:16
  311.0 9.7 %collective-permute-done.3 = f32[4,2]{0,1:T(2,128)S(1)} collective-permute-done((f32[4,2]{0,1:T(2,128)S(1)}, f32[4,2]{0,1:T(2,128)S(1)}, u32[]{:S(2)}, u32[]{:S(2)}) %collective-permute-start.3) | collective-permute-done | bytes 64 | tf_op jit(solution)/shard_map/ppermute | solution.py:16
  323.3 3.6 %fusion.2 = bf16[8,16,4096]{2,0,1:T(8,128)(2,1)S(1)} fusion(f32[16,8,4096]{2,1,0:T(8,128)} %get-tuple-element.67, f32[8,16,4096]{2,1,0:T(8,128)} %convert.4), kind=kLoop, calls=%fused_computation.20 | loop fusion | flops 3145728 | bytes 5242880 | tf_op jit(solution)/shard_map/convert_element_type | solution.py:135
  332.0 5.7 %scatter_fusion.1 = bf16[12,16,4096]{2,1,0:T(8,128)(2,1)} fusion(bf16[12,16,4096]{2,1,0:T(8,128)(2,1)} %broadcast_in_dim.97, s32[16]{0:T(128)S(1)} %fusion.5, bf16[16,16,4096]{2,1,0:T(8,128)(2,1)} %all-to-all-done), kind=kCustom, calls=%fused_computation.2 | custom fusion | bytes 6291520 | tf_op jit(solution)/shard_map/scatter | solution.py:88
  (212 shorter events, 163.4 us)
Async XLA Ops:
  7.2 7.3 %copy-start = (bf16[4096,288]{0,1:T(8,128)(2,1)S(1)}, bf16[4096,288]{0,1:T(8,128)(2,1)}, u32[]{:S(2)}) copy-start(bf16[4096,288]{0,1:T(8,128)(2,1)} %param.25) | copy-start | bytes 7077892
  7.2 4.0 %copy-start.2 = (bf16[128,4096]{1,0:T(8,128)(2,1)S(1)}, bf16[128,4096]{1,0:T(8,128)(2,1)}, u32[]{:S(2)}) copy-start(bf16[128,4096]{1,0:T(8,128)(2,1)} %param.20) | copy-start | bytes 3145732
  7.2 4.0 %copy-start.7 = (f32[4096]{0:T(1024)S(1)}, f32[4096]{0:T(1024)}, u32[]{:S(2)}) copy-start(f32[4096]{0:T(1024)} %param.24) | copy-start | bytes 49156
  7.2 33.3 %all-reduce.2.cloned.1.call-start = ((), (), s32[]{:S(2)}) async-start(), calls=%async_computation.2 | async-start | bytes 294912 | tf_op jit(solution)/shard_map/psum | solution.py:98
  11.2 2.7 copy-start.1
  14.4 1.5 copy-start.9
  14.5 1.7 copy-start.13
  22.1 243.7 %all-to-all-start.1 = ((bf16[16,3,4096]{2,1,0:T(4,128)(2,1)}), bf16[16,3,4096]{2,1,0:T(4,128)(2,1)}, u32[]{:S(2)}, u32[]{:S(2)}) async-start(bf16[16,3,4096]{2,1,0:T(4,128)(2,1)} %scatter_fusion.2), calls=%async_computation.1 | async-start | bytes 1048576 | tf_op jit(solution)/shard_map/all_to_all | solution.py:129
  29.5 2.9 copy-start.6
  29.6 11.7 %copy-start.10 = (f32[16]{0:T(128)S(1)}, f32[16]{0:T(128)}, u32[]{:S(2)}) copy-start(f32[16]{0:T(128)} %param.28) | copy-start | bytes 196
  29.6 11.7 %copy-start.11 = (f32[16]{0:T(128)S(1)}, f32[16]{0:T(128)}, u32[]{:S(2)}) copy-start(f32[16]{0:T(128)} %param.27) | copy-start | bytes 196
  44.0 4.6 %copy-start.5 = (f32[4096]{0:T(1024)S(1)}, f32[4096]{0:T(1024)}, u32[]{:S(2)}) copy-start(f32[4096]{0:T(1024)} %param.32) | copy-start | bytes 49156
  265.8 5.9 %copy-start.8 = (s32[4,2]{0,1:T(2,128)S(1)}, s32[4,2]{0,1:T(2,128)}, u32[]{:S(2)}) copy-start(s32[4,2]{0,1:T(2,128)} %param.36) | copy-start | bytes 100
  265.8 5.9 %copy-start.12 = (s32[8]{0:T(128)S(1)}, s32[8]{0:T(128)}, u32[]{:S(2)}) copy-start(s32[8]{0:T(128)} %param.35) | copy-start | bytes 100
  265.8 6.6 %copy-start.14 = (s32[128]{0:T(128)S(1)}, s32[128]{0:T(128)}, u32[]{:S(2)}) copy-start(s32[128]{0:T(128)} %param.37) | copy-start | bytes 1540
  265.8 7.0 %copy-start.4 = (bf16[128,4096]{1,0:T(8,128)(2,1)S(1)}, bf16[128,4096]{1,0:T(8,128)(2,1)}, u32[]{:S(2)}) copy-start(bf16[128,4096]{1,0:T(8,128)(2,1)} %param.21) | copy-start | bytes 3145732
  265.8 64.8 %all-to-all-start = ((bf16[16,16,4096]{2,1,0:T(8,128)(2,1)}), bf16[16,16,4096]{2,1,0:T(8,128)(2,1)}, u32[]{:S(2)}, u32[]{:S(2)}) async-start(bf16[16,16,4096]{2,1,0:T(8,128)(2,1)} %scatter_fusion), calls=%async_computation | async-start | bytes 4194304 | tf_op jit(solution)/shard_map/all_to_all | solution.py:128
  272.0 3.1 collective-permute-start
  275.1 9.2 %collective-permute-start.1 = (f32[4,2]{0,1:T(2,128)S(1)}, f32[4,2]{0,1:T(2,128)S(1)}, u32[]{:S(2)}, u32[]{:S(2)}) collective-permute-start(f32[4,2]{0,1:T(2,128)S(1)} %fusion.15), channel_id=1, source_target_pairs={{0,4},{2,6},{4,0},{6,2},{8,12},{10,14},{12,8},{14,10},{16,20},{18,... | collective-permute-start | bytes 104 | tf_op jit(solution)/shard_map/ppermute | solution.py:16
  284.3 22.4 %collective-permute-start.2 = (f32[4,2]{0,1:T(2,128)S(1)}, f32[4,2]{0,1:T(2,128)S(1)}, u32[]{:S(2)}, u32[]{:S(2)}) collective-permute-start(f32[4,2]{0,1:T(2,128)S(1)} %fusion.23), channel_id=1, source_target_pairs={{0,8},{2,10},{4,12},{6,14},{8,0},{10,2},{12,4},{14,6},{16,24},{18,... | collective-permute-start | bytes 104 | tf_op jit(solution)/shard_map/ppermute | solution.py:16
  306.7 14.1 %collective-permute-start.3 = (f32[4,2]{0,1:T(2,128)S(1)}, f32[4,2]{0,1:T(2,128)S(1)}, u32[]{:S(2)}, u32[]{:S(2)}) collective-permute-start(f32[4,2]{0,1:T(2,128)S(1)} %add.205), channel_id=1, source_target_pairs={{0,16},{2,18},{4,20},{6,22},{8,24},{10,26},{12,28},{14,30},{16,0},... | collective-permute-start | bytes 104 | tf_op jit(solution)/shard_map/ppermute | solution.py:16
  330.6 7.0 %copy-start.3 = (bf16[12,3,4096]{2,1,0:T(4,128)(2,1)}, bf16[12,3,4096]{2,1,0:T(4,128)(2,1)S(1)}, u32[]{:S(2)}) copy-start(bf16[12,3,4096]{2,1,0:T(4,128)(2,1)S(1)} %scatter_fusion.3) | copy-start | bytes 884740
Sparse Core Ops, SparseCore 0:
  16.1 24.4 all-reduce.1
